TPU v7x, 32 devices: a whole 2x2x4 slice. The times are simulated.
32 devices in a mesh: days: 2 (over y), sta: 8 (over z, x), win: 2 (over core).
Axes of the slice: x: 2, y: 2, z: 4, core: 2. Of those that a mesh axis runs over, the one named last changes fastest.
Arguments:
- phases: bfloat16 [48, 2048, 16], P(('days', 'win'), 'sta'), parts along dimension 0, may hold values from -3.140625 to 3.140625
- window_valid: int32 [48], P('days'), parts along dimension 0, may hold values 0 or 1
- freq_taper: float32 [2048], replicated, may hold values from 0.1 to 1.9
- pair_mask: int32 [8, 8], replicated, may hold values from 0 to 1, as said below
Outputs:
- correlations: float32 [32, 16, 512], P(('days', 'sta'), None, 'win'), parts along dimension 0
There are 2 independent parts, one for each index of `days`. A program takes and returns all parts, laid end to end along the dimension named above; an argument that names none is the same for every part. Nothing has to cross between parts.
Inputs may be any that keep to these rules, and one draw needn't show every extreme that they name: `pair_mask`: symmetric over the two block indices; every diagonal block is kept.
All inputs are finite; a program needn't handle non-finite values.
Results may differ from a plain program's by a relative error of at most 0.005.
Values may be sent and summed in bfloat16 or wider, within the bound.
A program may use at most 64 MiB of HBM per device.

v0:
```python
import math

import jax
import jax.numpy as jnp
from jax import lax
from jax.sharding import PartitionSpec as P

LAGS = 512


def lag_table(freq_bins, lag_count):
    freq_index = jnp.arange(freq_bins, dtype=jnp.int32)[:, None]
    lag_index = jnp.arange(lag_count, dtype=jnp.int32)[None, :] - lag_count // 2
    wrapped = jnp.mod(freq_index * lag_index, 2 * freq_bins)
    angle = wrapped.astype(jnp.float32) * (math.pi / freq_bins)
    return jnp.stack((jnp.cos(angle), -jnp.sin(angle))).astype(jnp.bfloat16)


def per_device(phases, window_valid, freq_taper, pair_mask):
    sta_count = lax.axis_size("sta")
    win_rows, band_bins, stations = phases.shape
    freq_bins = band_bins * sta_count
    recv_rows = stations // sta_count
    sta_index = lax.axis_index("sta")
    win_group = lax.axis_index("win")
    valid_count = jnp.sum(window_valid.astype(jnp.float32))
    norm_scale = 1.0 / jnp.sqrt(freq_bins * jnp.maximum(valid_count, 1.0))
    bin_weight = freq_taper * norm_scale
    group_valid = lax.dynamic_slice_in_dim(window_valid, win_group * win_rows, win_rows)
    group_weight = group_valid.astype(jnp.bfloat16)[:, None, None]
    own_f = phases.astype(jnp.float32)
    own_cos = jnp.cos(own_f).astype(jnp.bfloat16)
    own_sin = jnp.sin(own_f).astype(jnp.bfloat16)
    left_cos = own_cos * group_weight
    left_sin = own_sin * group_weight
    band_weight = lax.dynamic_slice_in_dim(bin_weight, sta_index * band_bins, band_bins)
    pair_re = jnp.einsum("wki,wkj->ijk", left_cos, own_cos, preferred_element_type=jnp.float32)
    pair_re = pair_re + jnp.einsum(
        "wki,wkj->ijk", left_sin, own_sin, preferred_element_type=jnp.float32
    )
    band_re = (pair_re * band_weight).astype(jnp.bfloat16)
    pair_im = jnp.einsum("wki,wkj->ijk", left_sin, own_cos, preferred_element_type=jnp.float32)
    pair_im = pair_im - jnp.einsum(
        "wki,wkj->ijk", left_cos, own_sin, preferred_element_type=jnp.float32
    )
    band_im = (pair_im * band_weight).astype(jnp.bfloat16)
    spectra = lax.all_to_all(
        jnp.stack((band_re, band_im)), "sta", split_axis=1, concat_axis=3, tiled=True
    )
    lag_count = LAGS
    transform = lag_table(freq_bins, lag_count)
    flat_spectra = spectra.reshape(2, recv_rows * stations, freq_bins)
    correlation = jnp.einsum(
        "cnk,ckt->nt", flat_spectra, transform, preferred_element_type=jnp.float32
    )
    block_row = lax.dynamic_index_in_dim(pair_mask, sta_index, 0, keepdims=False)
    station_row = jnp.repeat(block_row, recv_rows).astype(jnp.float32)
    receiver = sta_index * recv_rows + jnp.arange(recv_rows, dtype=jnp.int32)
    distinct = (receiver[:, None] != jnp.arange(stations, dtype=jnp.int32)[None, :]).astype(
        jnp.float32
    )
    pair_keep = station_row[None, :] * distinct
    correlation = correlation.reshape(recv_rows, stations, lag_count) * pair_keep[:, :, None]
    return lax.psum_scatter(correlation, "win", scatter_dimension=2, tiled=True)


def solution(mesh):
    return jax.shard_map(
        per_device,
        mesh=mesh,
        in_specs=(P(("days", "win"), "sta", None), P("days"), P(), P()),
        out_specs=P(("days", "sta"), None, "win"),
        check_vma=False,
    )
```

profile of v0, /device:TPU:0, one launch (start us, length us, event | category | flops | bytes accessed | tf_op | source)
XLA Modules:
  0.0 74.8 jit_solution(9505695054169387936)
XLA Ops:
  6.5 1.3 %convert_reduce_fusion = f32[]{:T(128)} fusion(s32[24]{0:T(128)} %param.5), kind=kLoop, calls=%fused_computation.32 | loop fusion | flops 47 | bytes 100 | tf_op jit(solution)/shard_map/reduce_sum | solution.py:26
  8.5 0.7 dynamic-slice_convert_fusion
  9.2 1.6 %fusion.12 = (bf16[12,256,16]{1,2,0:T(8,128)(2,1)S(1)}, bf16[12,256,16]{1,2,0:T(8,128)(2,1)S(1)}) fusion(bf16[12,256,16]{1,2,0:T(8,128)(2,1)} %param.4), kind=kLoop, calls=%fused_computation.24 | loop fusion | flops 147456 | bytes 294912 | tf_op jit(solution)/shard_map/convert_element_type | solution.py:33
  10.8 1.6 %broadcast_multiply_fusion.1 = (bf16[12,256,16]{1,2,0:T(8,128)(2,1)S(1)}, bf16[12,256,16]{1,2,0:T(8,128)(2,1)S(1)}) fusion(bf16[12]{0:T(256)(128)(2,1)S(1)} %dynamic-slice_convert_fusion, bf16[12,256,16]{1,2,0:T(8,128)(2,1)} %param.4), kind=kLoop, calls=%fused_computation.26 | loop fusion | flops 491520 | bytes 294936 | tf_op jit(solution)/shard_map/mul | solution.py:34
  12.4 1.0 %copy.35 = bf16[12,256,16]{0,2,1:T(8,128)(2,1)S(1)} copy(bf16[12,256,16]{1,2,0:T(8,128)(2,1)S(1)} %get-tuple-element.5) | data formatting | bytes 196608 | tf_op jit(solution)/shard_map/mul | solution.py:34
  13.5 1.9 %copy.36 = bf16[12,256,16]{2,0,1:T(8,128)(2,1)} copy(bf16[12,256,16]{1,2,0:T(8,128)(2,1)S(1)} %get-tuple-element.8) | data formatting | bytes 196608 | tf_op jit(solution)/shard_map/convert_element_type | solution.py:32
  15.4 1.0 %copy.37 = bf16[12,256,16]{0,2,1:T(8,128)(2,1)S(1)} copy(bf16[12,256,16]{1,2,0:T(8,128)(2,1)S(1)} %get-tuple-element.6) | data formatting | bytes 196608 | tf_op jit(solution)/shard_map/mul | solution.py:35
  16.4 0.9 %copy.38 = bf16[12,256,16]{2,0,1:T(8,128)(2,1)S(1)} copy(bf16[12,256,16]{1,2,0:T(8,128)(2,1)S(1)} %get-tuple-element.7) | data formatting | bytes 196608 | tf_op jit(solution)/shard_map/convert_element_type | solution.py:33
  17.3 0.0 copy-start
  17.4 3.3 %fusion.14 = f32[256,16,16]{2,1,0:T(8,128)} fusion(bf16[12,256,16]{0,2,1:T(8,128)(2,1)S(1)} %copy.35, bf16[12,256,16]{2,0,1:T(8,128)(2,1)} %copy.36), kind=kOutput, calls=%fused_computation.35 | convolution fusion | flops 1572864 | bytes 458752 | tf_op jit(solution)/shard_map/wki,wkj->ijk/dot_general | solution.py:37
  20.7 0.0 copy-done
  20.7 2.0 %fusion.15 = f32[256,16,16]{2,1,0:T(8,128)} fusion(bf16[12,256,16]{0,2,1:T(8,128)(2,1)S(1)} %copy.37, bf16[12,256,16]{2,0,1:T(8,128)(2,1)S(1)} %copy-done), kind=kOutput, calls=%fused_computation.36 | convolution fusion | flops 1572864 | bytes 458752 | tf_op jit(solution)/shard_map/wki,wkj->ijk/dot_general | solution.py:42
  22.7 0.8 %dynamic-slice_multiply_fusion = f32[256]{0:T(256)S(1)} fusion(f32[2048]{0:T(1024)} %param.6, s32[]{:T(128)S(6)} %select_n.31, f32[]{:T(128)S(6)} %sqrt.3), kind=kLoop, calls=%fused_computation.29 | loop fusion | flops 256 | bytes 2056 | tf_op jit(solution)/shard_map/mul | solution.py:28
  23.4 0.0 copy-start.1
  23.4 2.4 %fusion.7 = bf16[1,16,16,256]{2,1,3,0:T(8,128)(2,1)S(1)} fusion(f32[256,16,16]{2,1,0:T(8,128)} %fusion.14, bf16[12,256,16]{0,2,1:T(8,128)(2,1)S(1)} %copy.37, bf16[12,256,16]{2,0,1:T(8,128)(2,1)S(1)} %copy.38, f32[256]{0:T(256)S(1)} %dynamic-slice_multiply_fusion), kind=kOutput, calls=%fused_computation.16 | convolution fusion | flops 1769472 | bytes 590848 | tf_op jit(solution)/shard_map/wki,wkj->ijk/dot_general | solution.py:38
  25.9 0.0 copy-done.1
  25.9 0.7 fusion.8
  26.6 0.5 pad_maximum_fusion
  27.0 2.3 %copy.43 = bf16[2,16,16,256]{3,2,0,1:T(8,128)(2,1)} copy(bf16[2,16,16,256]{2,1,3,0:T(8,128)(2,1)S(1)} %pad_maximum_fusion) | data formatting | bytes 524288 | tf_op jit(solution)/shard_map/stack | solution.py:48
  29.3 7.3 %all-to-all-start = ((bf16[2,16,16,256]{3,2,0,1:T(8,128)(2,1)}), bf16[2,16,16,256]{3,2,0,1:T(8,128)(2,1)S(1)}, u32[]{:S(2)}, u32[]{:S(2)}) async-start(bf16[2,16,16,256]{3,2,0,1:T(8,128)(2,1)} %copy.43), calls=%async_computation | async-start | bytes 524288 | tf_op jit(solution)/shard_map/all_to_all | solution.py:47
  36.6 0.0 reduce-scatter.2.cloned.1.call-start
  36.7 0.7 convert_bitcast_fusion
  37.4 0.1 broadcast_in_dim.2
  37.4 0.1 convert_element_type.71
  37.5 0.1 compare_select_fusion
  37.6 18.1 %cosine_convert_fusion = (bf16[1,2048,512]{2,1,0:T(8,128)(2,1)S(1)}, bf16[1,2048,512]{2,1,0:T(8,128)(2,1)}) fusion(s32[512]{0:T(512)S(1)} %iota_add_fusion), kind=kLoop, calls=%fused_computation.8 | loop fusion | flops 17825792 | bytes 4196352 | tf_op jit(solution)/shard_map/convert
  55.7 0.0 all-to-all-done
  55.7 0.1 copy.47
  55.9 0.1 reshape.160
  56.0 2.9 %fusion.10 = f32[2,16,512]{2,1,0:T(8,128)} fusion(bf16[2,16,2,2048]{3,1,0,2:T(8,128)(2,1)S(1)} %bitcast.43, bf16[1,2048,512]{2,1,0:T(8,128)(2,1)} %get-tuple-element.10, bf16[1,2048,512]{2,1,0:T(8,128)(2,1)S(1)} %get-tuple-element.9, f32[2,16]{1,0:T(2,128)S(1)} %compare_select_fusion), kind=kOutput, calls=%fused_computation.19 | convolution fusion | flops 136331264 | bytes 4522112 | tf_op jit(solution)/shard_map/cnk,ckt->nt/dot_general | solution.py:53
  58.9 0.0 reduce-scatter.2.cloned.1.call-update
  58.9 9.1 %reduce-scatter.2.cloned.1.call-done = f32[2,16,256]{2,1,0:T(8,128)} async-done(((f32[2,16,512]{2,1,0:T(8,128)}), f32[2,16,256]{2,1,0:T(8,128)}) %reduce-scatter.2.cloned.1.call-update) | async-done | bytes 32784 | tf_op jit(solution)/shard_map/reduce_scatter | solution.py:64
  (2 shorter events, 0.0 us)
Async XLA Ops:
  17.3 3.3 %copy-start = (bf16[12,256,16]{2,0,1:T(8,128)(2,1)S(1)}, bf16[12,256,16]{2,0,1:T(8,128)(2,1)}, u32[]{:S(2)}) copy-start(bf16[12,256,16]{2,0,1:T(8,128)(2,1)} %copy.36) | copy-start | bytes 294916
  23.4 2.4 %copy-start.1 = (f32[256,16,16]{2,1,0:T(8,128)S(1)}, f32[256,16,16]{2,1,0:T(8,128)}, u32[]{:S(2)}) copy-start(f32[256,16,16]{2,1,0:T(8,128)} %fusion.15) | copy-start | bytes 786436
  29.3 26.4 %all-to-all-start = ((bf16[2,16,16,256]{3,2,0,1:T(8,128)(2,1)}), bf16[2,16,16,256]{3,2,0,1:T(8,128)(2,1)S(1)}, u32[]{:S(2)}, u32[]{:S(2)}) async-start(bf16[2,16,16,256]{3,2,0,1:T(8,128)(2,1)} %copy.43), calls=%async_computation | async-start | bytes 524288 | tf_op jit(solution)/shard_map/all_to_all | solution.py:47
  36.6 31.4 %reduce-scatter.2.cloned.1.call-start = ((), (), s32[]{:S(2)}) async-start(), calls=%async_computation.2 | async-start | bytes 98304 | tf_op jit(solution)/shard_map/reduce_scatter | solution.py:64
Sparse Core Ops, SparseCore 0:
  59.1 8.8 reduce-scatter.1
where the time goes:
time: 75.3 us; the launch traced here: 74.8 us
  other arithmetic  25.3 us (34%)
  between operations  14.2 us (19%)
  matrix products  11.3 us (15%)
  waiting for transfers between devices  9.08 us (12%)
  local copies, waits for them, and re-layouts  7.59 us (10%)
  starting transfers between devices  7.31 us (10%)
    another operation x1, other arithmetic  18.1 us
    reduce_scatter x1, waiting for transfers between devices, per_device(): return lax.psum_scatter(correlation, 'win', scatter_dimension=2, tiled=True)  9.07 us
    all_to_all x1, starting transfers between devices, per_device(): lax.all_to_all(jnp.stack((band_re, band_im)), 'sta', split_axis=1, concat...  7.28 us
    dot_general x1, matrix products, per_device(): jnp.einsum('wki,wkj->ijk', left_cos, own_cos, preferred_element_type=jnp....  3.32 us
    dot_general x1, matrix products, per_device(): jnp.einsum('cnk,ckt->nt', flat_spectra, transform, preferred_element_type...  2.92 us
    dot_general x1, matrix products, per_device(): jnp.einsum('wki,wkj->ijk', left_sin, own_sin, preferred_element_type=jnp....  2.42 us
    another operation x1, local copies, waits for them, and re-layouts, per_device(): jnp.stack((band_re, band_im))  2.28 us
    dot_general x1, matrix products, per_device(): jnp.einsum('wki,wkj->ijk', left_sin, own_cos, preferred_element_type=jnp....  1.98 us
  transfers between devices with their start and end apart: 2, of which 1 were waited for; matrix products, arithmetic and copies ran while one was open for 25% of the time, Pallas kernels for 0%

commit v1 on v0

--- a/solution.py
+++ b/solution.py
@@ -2,10 +2,226 @@
 
 import jax
 import jax.numpy as jnp
+import numpy as np
 from jax import lax
+from jax.experimental import pallas as pl
+from jax.experimental.pallas import tpu as pltpu
 from jax.sharding import PartitionSpec as P
 
 LAGS = 512
+MESH = pl.DeviceIdType.MESH
+
+
+def fit(function, degree):
+    nodes = np.polynomial.chebyshev.Chebyshev.interpolate(function, degree, domain=[0.0, math.pi**2])
+    return [float(c) for c in nodes.convert(kind=np.polynomial.Polynomial).coef]
+
+
+def sinc_of_square(y):
+    x = np.sqrt(y)
+    return np.sinc(x / math.pi)
+
+
+SIN_COEF = fit(sinc_of_square, 7)
+COS_COEF = fit(lambda y: np.cos(np.sqrt(y)), 8)
+
+
+def horner(coef, y):
+    total = jnp.full_like(y, coef[-1])
+    for c in coef[-2::-1]:
+        total = total * y + c
+    return total
+
+
+def cos_sin(x):
+    y = x * x
+    return horner(COS_COEF, y), x * horner(SIN_COEF, y)
+
+
+def fused_kernel(
+    phases_ref,
+    valid_ref,
+    taper_ref,
+    mask_ref,
+    out_ref,
+    cos_ref,
+    sin_ref,
+    spec_re,
+    spec_im,
+    lag_cos,
+    lag_sin,
+    own,
+    swap_out,
+    swap_in,
+    send,
+    recv,
+    swap_send_sem,
+    swap_recv_sem,
+    send_sem,
+    recv_sem,
+    *,
+    sta_count,
+):
+    days, sta, win = (lax.axis_index(a) for a in ("days", "sta", "win"))
+    win_rows, stations, band = phases_ref.shape
+    recv_rows = stations // sta_count
+    block = recv_rows * stations
+    freq_bins = band * sta_count
+    half = LAGS // 2
+
+    barrier = pltpu.get_barrier_semaphore()
+    pl.semaphore_signal(barrier, inc=1, device_id=(days, sta, 1 - win), device_id_type=MESH)
+    for step in range(1, sta_count):
+        peer = lax.rem(sta + step, sta_count)
+        pl.semaphore_signal(barrier, inc=1, device_id=(days, peer, win), device_id_type=MESH)
+
+    @pl.loop(0, win_rows)
+    def _(w):
+        weight = valid_ref[win * win_rows + w].astype(jnp.float32)
+        c, s = cos_sin(phases_ref[w].astype(jnp.float32))
+        cos_ref[w] = c.astype(jnp.bfloat16).astype(jnp.float32) * weight
+        sin_ref[w] = s.astype(jnp.bfloat16).astype(jnp.float32) * weight
+
+    rows = 16
+    lag = lax.broadcasted_iota(jnp.int32, (rows, LAGS), 1) - half
+    sub = lax.broadcasted_iota(jnp.int32, (rows, LAGS), 0)
+
+    @pl.loop(0, band // rows)
+    def _(b):
+        k = sub + (sta * band + b * rows)
+        turn = ((k * lag + freq_bins) & (2 * freq_bins - 1)) - freq_bins
+        c, s = cos_sin(turn.astype(jnp.float32) * (math.pi / freq_bins))
+        at = pl.ds(pl.multiple_of(b * rows, rows), rows)
+        lag_cos[at, :] = c.astype(jnp.bfloat16)
+        lag_sin[at, :] = (-s).astype(jnp.bfloat16)
+
+    count = valid_ref[0]
+    for w in range(1, valid_ref.shape[0]):
+        count = count + valid_ref[w]
+    count = jnp.full((1, 128), count, jnp.int32).astype(jnp.float32)
+    norm = 1.0 / jnp.sqrt(freq_bins * jnp.maximum(count, 1.0))
+    lane_rows = band // 128
+    weight = jnp.concatenate(
+        [taper_ref[pl.ds(sta * lane_rows + r, 1), :] * norm for r in range(lane_rows)], axis=1
+    )
+
+    @pl.loop(0, stations // 2)
+    def _(p):
+        re = [jnp.zeros((stations, band), jnp.float32) for _ in range(2)]
+        im = [jnp.zeros((stations, band), jnp.float32) for _ in range(2)]
+        for w in range(win_rows):
+            cj, sj = cos_ref[w], sin_ref[w]
+            for q in range(2):
+                ci = cos_ref[w, pl.ds(2 * p + q, 1), :]
+                si = sin_ref[w, pl.ds(2 * p + q, 1), :]
+                re[q] = re[q] + (ci * cj + si * sj)
+                im[q] = im[q] + (si * cj - ci * sj)
+        for q in range(2):
+            at = pl.ds(pl.multiple_of((2 * p + q) * stations, stations), stations)
+            spec_re[at, :] = (re[q] * weight).astype(jnp.bfloat16)
+            spec_im[at, :] = (im[q] * weight).astype(jnp.bfloat16)
+
+    def to_lags(which):
+        at = pl.ds(pl.multiple_of(which * half, half), half)
+        part = jnp.dot(spec_re[...], lag_cos[:, at], preferred_element_type=jnp.float32)
+        return part + jnp.dot(spec_im[...], lag_sin[:, at], preferred_element_type=jnp.float32)
+
+    other = to_lags(1 - win).astype(jnp.bfloat16)
+    for b in range(sta_count):
+        swap_out[b] = other[b * block : (b + 1) * block]
+    pl.semaphore_wait(barrier, sta_count)
+
+    def swap(step):
+        peer = lax.rem(sta + step, sta_count)
+        return pltpu.make_async_remote_copy(
+            src_ref=swap_out.at[peer],
+            dst_ref=swap_in.at[peer],
+            send_sem=swap_send_sem.at[step],
+            recv_sem=swap_recv_sem.at[step],
+            device_id=(days, sta, 1 - win),
+            device_id_type=MESH,
+        )
+
+    def scatter(step):
+        peer = lax.rem(sta + step, sta_count)
+        return pltpu.make_async_remote_copy(
+            src_ref=send.at[peer],
+            dst_ref=recv.at[step],
+            send_sem=send_sem.at[step],
+            recv_sem=recv_sem.at[step],
+            device_id=(days, peer, win),
+            device_id_type=MESH,
+        )
+
+    order = sorted(range(1, sta_count), key=lambda n: abs(n - sta_count // 2)) + [0]
+    for step in order:
+        swap(step).start()
+    mine = to_lags(win)
+    for b in range(sta_count):
+        own[b] = mine[b * block : (b + 1) * block]
+    for step in order:
+        peer = lax.rem(sta + step, sta_count)
+        swap(step).wait_recv()
+        total = own[peer] + swap_in[peer].astype(jnp.float32)
+        if step:
+            send[peer] = total.astype(jnp.bfloat16)
+            scatter(step).start()
+    for step in order[::-1][1:]:
+        scatter(step).wait_recv()
+        total = total + recv[step].astype(jnp.float32)
+
+    source = lax.broadcasted_iota(jnp.int32, (stations, half), 0)
+    keep = jnp.zeros((stations, half), jnp.float32)
+    for b in range(sta_count):
+        keep = jnp.where(source // recv_rows == b, mask_ref[sta, b].astype(jnp.float32), keep)
+    for r in range(recv_rows):
+        pair_keep = jnp.where(source == sta * recv_rows + r, 0.0, keep)
+        out_ref[r] = total[r * stations : (r + 1) * stations] * pair_keep
+    for step in order:
+        swap(step).wait_send()
+        if step:
+            scatter(step).wait_send()
+
+
+def fused(phases, window_valid, freq_taper, pair_mask):
+    sta_count = lax.axis_size("sta")
+    win_rows, band, stations = phases.shape
+    recv_rows = stations // sta_count
+    block = recv_rows * stations
+    pairs = stations * stations
+    half = LAGS // 2
+    f32, bf16, vmem = jnp.float32, jnp.bfloat16, pltpu.VMEM
+    in_vmem, in_smem = pl.BlockSpec(memory_space=pltpu.VMEM), pl.BlockSpec(memory_space=pltpu.SMEM)
+    return pl.pallas_call(
+        lambda *refs: fused_kernel(*refs, sta_count=sta_count),
+        name="fused",
+        out_shape=jax.ShapeDtypeStruct((recv_rows, stations, half), f32),
+        in_specs=[in_vmem, in_smem, in_vmem, in_smem],
+        out_specs=in_vmem,
+        scratch_shapes=[
+            vmem((win_rows, stations, band), f32),
+            vmem((win_rows, stations, band), f32),
+            vmem((pairs, band), bf16),
+            vmem((pairs, band), bf16),
+            vmem((band, LAGS), bf16),
+            vmem((band, LAGS), bf16),
+            vmem((sta_count, block, half), f32),
+            vmem((sta_count, block, half), bf16),
+            vmem((sta_count, block, half), bf16),
+            vmem((sta_count, block, half), bf16),
+            vmem((sta_count, block, half), bf16),
+            pltpu.SemaphoreType.DMA((sta_count,)),
+            pltpu.SemaphoreType.DMA((sta_count,)),
+            pltpu.SemaphoreType.DMA((sta_count,)),
+            pltpu.SemaphoreType.DMA((sta_count,)),
+        ],
+        compiler_params=pltpu.CompilerParams(collective_id=0, has_side_effects=True),
+    )(
+        jnp.transpose(phases, (0, 2, 1)),
+        window_valid,
+        freq_taper.reshape(-1, 128),
+        pair_mask,
+    )
 
 
 def lag_table(freq_bins, lag_count):
@@ -65,8 +281,16 @@
 
 
 def solution(mesh):
+    def body(phases, window_valid, freq_taper, pair_mask):
+        win_rows, band, stations = phases.shape
+        sta_count, win_count = mesh.shape["sta"], mesh.shape["win"]
+        power = band * sta_count & (band * sta_count - 1) == 0
+        if band % 128 == 0 and stations % 16 == 0 and win_count == 2 and power:
+            return fused(phases, window_valid, freq_taper, pair_mask)
+        return per_device(phases, window_valid, freq_taper, pair_mask)
+
     return jax.shard_map(
-        per_device,
+        body,
         mesh=mesh,
         in_specs=(P(("days", "win"), "sta", None), P("days"), P(), P()),
         out_specs=P(("days", "sta"), None, "win"),

time: 75.3 us -> 16.2 us (0.22)
  other arithmetic: 25.3 us -> 0 us
  Pallas kernels: 0 us -> 14.6 us
  between operations: 14.2 us -> 0.01 us
  matrix products: 11.3 us -> 0 us
  waiting for transfers between devices: 9.08 us -> 0 us
  starting transfers between devices: 7.31 us -> 0 us
  local copies, waits for them, and re-layouts: 7.59 us -> 1.38 us
    another operation x2 -> x0, other arithmetic: 18.6 us -> none
    pallas_call x0 -> x1, Pallas kernels: none -> 14.6 us  [fused(): pl.pallas_call(lambda *refs: fused_kernel(*refs, sta_count=sta_count), na...]
    dot_general x5 -> x0, matrix products: 11.3 us -> none  [the longest x1 3.32 us: per_device(): jnp.einsum('wki,wkj->ijk', left_cos, own_cos, preferred_element_type=jnp....]
    reduce_scatter x1 -> x0, waiting for transfers between devices: 9.07 us -> none  [per_device(): return lax.psum_scatter(correlation, 'win', scatter_dimension=2, tiled=True)]
    all_to_all x1 -> x0, starting transfers between devices: 7.28 us -> none  [per_device(): lax.all_to_all(jnp.stack((band_re, band_im)), 'sta', split_axis=1, concat...]
    convert_element_type x3 -> x0, other arithmetic: 3.02 us -> none  [the longest x1 1.59 us: per_device(): own_sin = jnp.sin(own_f).astype(jnp.bfloat16)]
    convert_element_type x3 -> x0, local copies, waits for them, and re-layouts: 2.91 us -> none  [the longest x1 1.88 us: per_device(): own_cos = jnp.cos(own_f).astype(jnp.bfloat16)]
    mul x3 -> x0, other arithmetic: 2.46 us -> none  [the longest x1 1.63 us: per_device(): left_cos = own_cos * group_weight]
  transfers between devices with their start and end apart: 2 -> 0, of which waited for: 1 -> 0; matrix products, arithmetic and copies ran while one was open for 25% -> 0% of each run, Pallas kernels for 0% -> 0%
where the time goes in v1:
time: 16.2 us; the launch traced here: 16 us
  Pallas kernels  14.6 us (90%)
  local copies, waits for them, and re-layouts  1.38 us (9%)
    pallas_call x1, Pallas kernels, fused(): pl.pallas_call(lambda *refs: fused_kernel(*refs, sta_count=sta_count), na...  14.6 us
    unnamed x1, local copies, waits for them, and re-layouts  1.38 us

profile of v1, /device:TPU:0, one launch (start us, length us, event | category | flops | bytes accessed | tf_op | source)
XLA Modules:
  0.0 16.0 jit_solution(2820910870433537454)
XLA Ops:
  0.0 14.6 %fused.1 = f32[2,16,256]{2,1,0:T(8,128)} custom-call(bf16[12,16,256]{2,1,0:T(8,128)(2,1)} %bitcast.2, s32[24]{0:T(128)} %refs_1_.1, f32[16,128]{1,0:T(8,128)} %bitcast.3, s32[8,8]{1,0:T(8,128)} %refs_3_.1), custom_call_target="tpu_custom_call" | custom-call | tf_op jit(solution)/shard_map/fused/pallas_call | solution.py:195
  14.6 1.4 %copy.6 = f32[2,16,256]{2,1,0:T(8,128)} copy(f32[2,16,256]{2,1,0:T(8,128)} %fused.1) | data formatting | bytes 65536

commit v2 on v1

--- a/solution.py
+++ b/solution.py
@@ -39,11 +39,16 @@
 
 
 def fused_kernel(
+    phases_hbm,
+    valid_hbm,
+    taper_hbm,
+    mask_hbm,
+    out_ref,
     phases_ref,
     valid_ref,
     taper_ref,
     mask_ref,
-    out_ref,
+    load_sem,
     cos_ref,
     sin_ref,
     spec_re,
@@ -63,24 +68,37 @@
     sta_count,
 ):
     days, sta, win = (lax.axis_index(a) for a in ("days", "sta", "win"))
-    win_rows, stations, band = phases_ref.shape
+    win_rows, stations, band = phases_hbm.shape
     recv_rows = stations // sta_count
     block = recv_rows * stations
     freq_bins = band * sta_count
     half = LAGS // 2
 
+    loads = [
+        pltpu.make_async_copy(source, target, load_sem.at[n])
+        for n, (source, target) in enumerate(
+            (
+                (phases_hbm, phases_ref),
+                (valid_hbm, valid_ref),
+                (taper_hbm, taper_ref),
+                (mask_hbm, mask_ref),
+            )
+        )
+    ]
+    for load in loads:
+        load.start()
+    def across(step):
+        peer = sta
+        for bit in range(step.bit_length()):
+            if step >> bit & 1:
+                peer = peer + 2**bit * (1 - 2 * lax.rem(sta // 2**bit, 2))
+        return peer
+
     barrier = pltpu.get_barrier_semaphore()
     pl.semaphore_signal(barrier, inc=1, device_id=(days, sta, 1 - win), device_id_type=MESH)
-    for step in range(1, sta_count):
-        peer = lax.rem(sta + step, sta_count)
+    for step in range(sta_count - 1, 0, -1):
+        peer = across(step)
         pl.semaphore_signal(barrier, inc=1, device_id=(days, peer, win), device_id_type=MESH)
-
-    @pl.loop(0, win_rows)
-    def _(w):
-        weight = valid_ref[win * win_rows + w].astype(jnp.float32)
-        c, s = cos_sin(phases_ref[w].astype(jnp.float32))
-        cos_ref[w] = c.astype(jnp.bfloat16).astype(jnp.float32) * weight
-        sin_ref[w] = s.astype(jnp.bfloat16).astype(jnp.float32) * weight
 
     rows = 16
     lag = lax.broadcasted_iota(jnp.int32, (rows, LAGS), 1) - half
@@ -94,6 +112,16 @@
         at = pl.ds(pl.multiple_of(b * rows, rows), rows)
         lag_cos[at, :] = c.astype(jnp.bfloat16)
         lag_sin[at, :] = (-s).astype(jnp.bfloat16)
+
+    for load in loads:
+        load.wait()
+
+    @pl.loop(0, win_rows)
+    def _(w):
+        weight = valid_ref[win * win_rows + w].astype(jnp.float32)
+        c, s = cos_sin(phases_ref[w].astype(jnp.float32))
+        cos_ref[w] = c.astype(jnp.bfloat16).astype(jnp.float32) * weight
+        sin_ref[w] = s.astype(jnp.bfloat16).astype(jnp.float32) * weight
 
     count = valid_ref[0]
     for w in range(1, valid_ref.shape[0]):
@@ -132,7 +160,7 @@
     pl.semaphore_wait(barrier, sta_count)
 
     def swap(step):
-        peer = lax.rem(sta + step, sta_count)
+        peer = across(step)
         return pltpu.make_async_remote_copy(
             src_ref=swap_out.at[peer],
             dst_ref=swap_in.at[peer],
@@ -143,7 +171,7 @@
         )
 
     def scatter(step):
-        peer = lax.rem(sta + step, sta_count)
+        peer = across(step)
         return pltpu.make_async_remote_copy(
             src_ref=send.at[peer],
             dst_ref=recv.at[step],
@@ -153,20 +181,20 @@
             device_id_type=MESH,
         )
 
-    order = sorted(range(1, sta_count), key=lambda n: abs(n - sta_count // 2)) + [0]
+    order = range(sta_count - 1, -1, -1)
     for step in order:
         swap(step).start()
     mine = to_lags(win)
     for b in range(sta_count):
         own[b] = mine[b * block : (b + 1) * block]
     for step in order:
-        peer = lax.rem(sta + step, sta_count)
+        peer = across(step)
         swap(step).wait_recv()
         total = own[peer] + swap_in[peer].astype(jnp.float32)
         if step:
             send[peer] = total.astype(jnp.bfloat16)
             scatter(step).start()
-    for step in order[::-1][1:]:
+    for step in range(1, sta_count):
         scatter(step).wait_recv()
         total = total + recv[step].astype(jnp.float32)
 
@@ -191,14 +219,18 @@
     pairs = stations * stations
     half = LAGS // 2
     f32, bf16, vmem = jnp.float32, jnp.bfloat16, pltpu.VMEM
-    in_vmem, in_smem = pl.BlockSpec(memory_space=pltpu.VMEM), pl.BlockSpec(memory_space=pltpu.SMEM)
     return pl.pallas_call(
         lambda *refs: fused_kernel(*refs, sta_count=sta_count),
         name="fused",
         out_shape=jax.ShapeDtypeStruct((recv_rows, stations, half), f32),
-        in_specs=[in_vmem, in_smem, in_vmem, in_smem],
-        out_specs=in_vmem,
+        in_specs=[pl.BlockSpec(memory_space=pltpu.HBM)] * 4,
+        out_specs=pl.BlockSpec(memory_space=pltpu.VMEM),
         scratch_shapes=[
+            vmem((win_rows, stations, band), bf16),
+            pltpu.SMEM(window_valid.shape, jnp.int32),
+            vmem((freq_taper.shape[0] // 128, 128), f32),
+            pltpu.SMEM(pair_mask.shape, jnp.int32),
+            pltpu.SemaphoreType.DMA((4,)),
             vmem((win_rows, stations, band), f32),
             vmem((win_rows, stations, band), f32),
             vmem((pairs, band), bf16),
@@ -215,12 +247,19 @@
             pltpu.SemaphoreType.DMA((sta_count,)),
             pltpu.SemaphoreType.DMA((sta_count,)),
         ],
-        compiler_params=pltpu.CompilerParams(collective_id=0, has_side_effects=True),
+        compiler_params=pltpu.CompilerParams(
+            collective_id=0, has_side_effects=True, vmem_limit_bytes=16 * 2**20
+        ),
     )(
-        jnp.transpose(phases, (0, 2, 1)),
-        window_valid,
-        freq_taper.reshape(-1, 128),
-        pair_mask,
+        *(
+            pltpu.with_memory_space_constraint(a, pltpu.HBM)
+            for a in (
+                jnp.transpose(phases, (0, 2, 1)),
+                window_valid,
+                freq_taper.reshape(-1, 128),
+                pair_mask,
+            )
+        )
     )
 
 
@@ -284,7 +323,7 @@
     def body(phases, window_valid, freq_taper, pair_mask):
         win_rows, band, stations = phases.shape
         sta_count, win_count = mesh.shape["sta"], mesh.shape["win"]
-        power = band * sta_count & (band * sta_count - 1) == 0
+        power = band * sta_count & (band * sta_count - 1) == 0 and sta_count & (sta_count - 1) == 0
         if band % 128 == 0 and stations % 16 == 0 and win_count == 2 and power:
             return fused(phases, window_valid, freq_taper, pair_mask)
         return per_device(phases, window_valid, freq_taper, pair_mask)

time: 16.2 us -> 12.7 us (0.78)
  Pallas kernels: 14.6 us -> 11.9 us
  local copies, waits for them, and re-layouts: 1.38 us -> 0.62 us
    pallas_call x1, Pallas kernels: 14.6 us -> 11.9 us  [fused(): pl.pallas_call(lambda *refs: fused_kernel(*refs, sta_count=sta_count), na...]
    unnamed x1, local copies, waits for them, and re-layouts: 1.38 us -> 0.62 us
where the time goes in v2:
time: 12.7 us; the launch traced here: 12.5 us
  Pallas kernels  11.9 us (94%)
  local copies, waits for them, and re-layouts  0.62 us (5%)
    pallas_call x1, Pallas kernels, fused(): pl.pallas_call(lambda *refs: fused_kernel(*refs, sta_count=sta_count), na...  11.9 us
    unnamed x1, local copies, waits for them, and re-layouts  0.62 us

profile of v2, /device:TPU:0, one launch (start us, length us, event | category | flops | bytes accessed | tf_op | source)
XLA Modules:
  0.0 12.5 jit_solution(443911259232334902)
XLA Ops:
  0.0 11.9 %fused.1 = f32[2,16,256]{2,1,0:T(8,128)S(1)} custom-call(bf16[12,16,256]{2,1,0:T(8,128)(2,1)} %bitcast.2, s32[24]{0:T(128)} %refs_1_.1, f32[16,128]{1,0:T(8,128)} %bitcast.3, s32[8,8]{1,0:T(8,128)} %refs_3_.1), custom_call_target="tpu_custom_call" | custom-call | tf_op jit(solution)/shard_map/fused/pallas_call | solution.py:222
  11.9 0.6 %copy.6 = f32[2,16,256]{2,1,0:T(8,128)} copy(f32[2,16,256]{2,1,0:T(8,128)S(1)} %fused.1) | data formatting | bytes 65536

commit v3 on v2

--- a/solution.py
+++ b/solution.py
@@ -64,6 +64,7 @@
     swap_recv_sem,
     send_sem,
     recv_sem,
+    ready,
     *,
     sta_count,
 ):
@@ -88,17 +89,16 @@
     for load in loads:
         load.start()
     def across(step):
-        peer = sta
-        for bit in range(step.bit_length()):
-            if step >> bit & 1:
-                peer = peer + 2**bit * (1 - 2 * lax.rem(sta // 2**bit, 2))
-        return peer
+        bits = [2**n for n in range((sta_count - 1).bit_length())]
+        return sum(lax.rem(lax.div(sta, n) + lax.div(jnp.int32(step), n), 2) * n for n in bits)
 
     barrier = pltpu.get_barrier_semaphore()
-    pl.semaphore_signal(barrier, inc=1, device_id=(days, sta, 1 - win), device_id_type=MESH)
     for step in range(sta_count - 1, 0, -1):
-        peer = across(step)
-        pl.semaphore_signal(barrier, inc=1, device_id=(days, peer, win), device_id_type=MESH)
+        pl.semaphore_signal(barrier, inc=1, device_id=(days, across(step), 1), device_id_type=MESH)
+
+    @pl.when(win == 1)
+    def _():
+        pl.semaphore_signal(barrier, inc=1, device_id=(days, sta, 0), device_id_type=MESH)
 
     rows = 16
     lag = lax.broadcasted_iota(jnp.int32, (rows, LAGS), 1) - half
@@ -113,6 +113,11 @@
         lag_cos[at, :] = c.astype(jnp.bfloat16)
         lag_sin[at, :] = (-s).astype(jnp.bfloat16)
 
+    @pl.when(win == 0)
+    def _():
+        pl.semaphore_wait(barrier, 1)
+        pl.semaphore_signal(ready, inc=1, device_id=(days, sta, 1), device_id_type=MESH)
+
     for load in loads:
         load.wait()
 
@@ -133,37 +138,10 @@
         [taper_ref[pl.ds(sta * lane_rows + r, 1), :] * norm for r in range(lane_rows)], axis=1
     )
 
-    @pl.loop(0, stations // 2)
-    def _(p):
-        re = [jnp.zeros((stations, band), jnp.float32) for _ in range(2)]
-        im = [jnp.zeros((stations, band), jnp.float32) for _ in range(2)]
-        for w in range(win_rows):
-            cj, sj = cos_ref[w], sin_ref[w]
-            for q in range(2):
-                ci = cos_ref[w, pl.ds(2 * p + q, 1), :]
-                si = sin_ref[w, pl.ds(2 * p + q, 1), :]
-                re[q] = re[q] + (ci * cj + si * sj)
-                im[q] = im[q] + (si * cj - ci * sj)
-        for q in range(2):
-            at = pl.ds(pl.multiple_of((2 * p + q) * stations, stations), stations)
-            spec_re[at, :] = (re[q] * weight).astype(jnp.bfloat16)
-            spec_im[at, :] = (im[q] * weight).astype(jnp.bfloat16)
-
-    def to_lags(which):
-        at = pl.ds(pl.multiple_of(which * half, half), half)
-        part = jnp.dot(spec_re[...], lag_cos[:, at], preferred_element_type=jnp.float32)
-        return part + jnp.dot(spec_im[...], lag_sin[:, at], preferred_element_type=jnp.float32)
-
-    other = to_lags(1 - win).astype(jnp.bfloat16)
-    for b in range(sta_count):
-        swap_out[b] = other[b * block : (b + 1) * block]
-    pl.semaphore_wait(barrier, sta_count)
-
     def swap(step):
-        peer = across(step)
         return pltpu.make_async_remote_copy(
-            src_ref=swap_out.at[peer],
-            dst_ref=swap_in.at[peer],
+            src_ref=swap_out.at[step],
+            dst_ref=swap_in.at[step],
             send_sem=swap_send_sem.at[step],
             recv_sem=swap_recv_sem.at[step],
             device_id=(days, sta, 1 - win),
@@ -181,16 +159,64 @@
             device_id_type=MESH,
         )
 
+    def cross(step):
+        first = across(step) * recv_rows
+        re = [jnp.zeros((stations, band), jnp.float32) for _ in range(recv_rows)]
+        im = [jnp.zeros((stations, band), jnp.float32) for _ in range(recv_rows)]
+        for w in range(win_rows):
+            cj, sj = cos_ref[w], sin_ref[w]
+            for q in range(recv_rows):
+                ci = cos_ref[w, pl.ds(first + q, 1), :]
+                si = sin_ref[w, pl.ds(first + q, 1), :]
+                re[q] = re[q] + (ci * cj + si * sj)
+                im[q] = im[q] + (si * cj - ci * sj)
+        at = pl.ds(pl.multiple_of(first * stations, block), block)
+        made = [
+            jnp.concatenate([(x * weight).astype(jnp.bfloat16) for x in part], axis=0)
+            for part in (re, im)
+        ]
+        spec_re[at, :], spec_im[at, :] = made
+        return made
+
+    def to_lags(re, im, which):
+        at = pl.ds(pl.multiple_of(which * half, half), half)
+        part = jnp.dot(re, lag_cos[:, at], preferred_element_type=jnp.float32)
+        return part + jnp.dot(im, lag_sin[:, at], preferred_element_type=jnp.float32)
+
+    def pack(step, re, im):
+        swap_out[step] = to_lags(re, im, 1 - win).astype(jnp.bfloat16)
+
+    @pl.when(win == 1)
+    def _():
+        pl.semaphore_wait(ready, 1)
+
+    def chunk(n, before):
+        step = sta_count - 1 - n
+        pack(step + 1, *before)
+        made = cross(step)
+        swap(step + 1).start()
+        return made
+
+    pack(0, *lax.fori_loop(1, sta_count, chunk, cross(sta_count - 1)))
+    mine = to_lags(spec_re[...], spec_im[...], win)
+    swap(0).start()
     order = range(sta_count - 1, -1, -1)
-    for step in order:
-        swap(step).start()
-    mine = to_lags(win)
     for b in range(sta_count):
         own[b] = mine[b * block : (b + 1) * block]
+
+    @pl.when(win == 1)
+    def _():
+        pl.semaphore_wait(barrier, 2 * (sta_count - 1))
+        pl.semaphore_signal(ready, inc=1, device_id=(days, sta, 0), device_id_type=MESH)
+
+    @pl.when(win == 0)
+    def _():
+        pl.semaphore_wait(ready, 1)
+
     for step in order:
         peer = across(step)
         swap(step).wait_recv()
-        total = own[peer] + swap_in[peer].astype(jnp.float32)
+        total = own[peer] + swap_in[step].astype(jnp.float32)
         if step:
             send[peer] = total.astype(jnp.bfloat16)
             scatter(step).start()
@@ -246,6 +272,7 @@
             pltpu.SemaphoreType.DMA((sta_count,)),
             pltpu.SemaphoreType.DMA((sta_count,)),
             pltpu.SemaphoreType.DMA((sta_count,)),
+            pltpu.SemaphoreType.REGULAR,
         ],
         compiler_params=pltpu.CompilerParams(
             collective_id=0, has_side_effects=True, vmem_limit_bytes=16 * 2**20

time: 12.7 us -> 12.2 us (0.961)
  Pallas kernels: 11.9 us -> 11.4 us
    pallas_call x1, Pallas kernels: 11.9 us -> 11.4 us  [fused(): pl.pallas_call(lambda *refs: fused_kernel(*refs, sta_count=sta_count), na...]
where the time goes in v3:
time: 12.2 us; the launch traced here: 12.1 us
  Pallas kernels  11.4 us (93%)
  local copies, waits for them, and re-layouts  0.62 us (5%)
    pallas_call x1, Pallas kernels, fused(): pl.pallas_call(lambda *refs: fused_kernel(*refs, sta_count=sta_count), na...  11.4 us
    unnamed x1, local copies, waits for them, and re-layouts  0.62 us

profile of v3, /device:TPU:0, one launch (start us, length us, event | category | flops | bytes accessed | tf_op | source)
XLA Modules:
  0.0 12.1 jit_solution(7354214164079636816)
XLA Ops:
  0.0 11.4 %fused.1 = f32[2,16,256]{2,1,0:T(8,128)S(1)} custom-call(bf16[12,16,256]{2,1,0:T(8,128)(2,1)} %bitcast.2, s32[24]{0:T(128)} %refs_1_.1, f32[16,128]{1,0:T(8,128)} %bitcast.3, s32[8,8]{1,0:T(8,128)} %refs_3_.1), custom_call_target="tpu_custom_call" | custom-call | tf_op jit(solution)/shard_map/fused/pallas_call | solution.py:248
  11.4 0.6 %copy.6 = f32[2,16,256]{2,1,0:T(8,128)} copy(f32[2,16,256]{2,1,0:T(8,128)S(1)} %fused.1) | data formatting | bytes 65536

commit v4 on v3

--- a/solution.py
+++ b/solution.py
@@ -60,6 +60,10 @@
     swap_in,
     send,
     recv,
+    beside_out,
+    beside_in,
+    beside_send_sem,
+    beside_recv_sem,
     swap_send_sem,
     swap_recv_sem,
     send_sem,
@@ -94,7 +98,9 @@
 
     barrier = pltpu.get_barrier_semaphore()
     for step in range(sta_count - 1, 0, -1):
-        pl.semaphore_signal(barrier, inc=1, device_id=(days, across(step), 1), device_id_type=MESH)
+        pl.semaphore_signal(
+            barrier, inc=1, device_id=(days, across(step), int(step > 1)), device_id_type=MESH
+        )
 
     @pl.when(win == 1)
     def _():
@@ -115,7 +121,7 @@
 
     @pl.when(win == 0)
     def _():
-        pl.semaphore_wait(barrier, 1)
+        pl.semaphore_wait(barrier, 3)
         pl.semaphore_signal(ready, inc=1, device_id=(days, sta, 1), device_id_type=MESH)
 
     for load in loads:
@@ -156,6 +162,16 @@
             send_sem=send_sem.at[step],
             recv_sem=recv_sem.at[step],
             device_id=(days, peer, win),
+            device_id_type=MESH,
+        )
+
+    def beside(slot):
+        return pltpu.make_async_remote_copy(
+            src_ref=beside_out.at[slot],
+            dst_ref=beside_in.at[slot],
+            send_sem=beside_send_sem.at[slot],
+            recv_sem=beside_recv_sem.at[slot],
+            device_id=(days, across(1), win),
             device_id_type=MESH,
         )
 
@@ -200,27 +216,40 @@
     pack(0, *lax.fori_loop(1, sta_count, chunk, cross(sta_count - 1)))
     mine = to_lags(spec_re[...], spec_im[...], win)
     swap(0).start()
-    order = range(sta_count - 1, -1, -1)
     for b in range(sta_count):
         own[b] = mine[b * block : (b + 1) * block]
 
+    def over_groups(step):
+        swap(step).wait_recv()
+        return own[across(step)] + swap_in[step].astype(jnp.float32)
+
+    for slot, step in enumerate((7, 5)):
+        beside_out[slot] = over_groups(step).astype(jnp.bfloat16)
+        beside(slot).start()
+    far = [over_groups(step) for step in (6, 4)]
+    for step in (1, 3, 2):
+        send[across(step)] = over_groups(step).astype(jnp.bfloat16)
+    scatter(1).start()
+    total = over_groups(0)
+
     @pl.when(win == 1)
     def _():
-        pl.semaphore_wait(barrier, 2 * (sta_count - 1))
+        pl.semaphore_wait(barrier, 2 * (sta_count - 2))
         pl.semaphore_signal(ready, inc=1, device_id=(days, sta, 0), device_id_type=MESH)
 
     @pl.when(win == 0)
     def _():
         pl.semaphore_wait(ready, 1)
 
-    for step in order:
-        peer = across(step)
-        swap(step).wait_recv()
-        total = own[peer] + swap_in[step].astype(jnp.float32)
-        if step:
-            send[peer] = total.astype(jnp.bfloat16)
-            scatter(step).start()
-    for step in range(1, sta_count):
+    for slot, step in enumerate((6, 4)):
+        beside(slot).wait_recv()
+        chunk_sum = far[slot] + beside_in[slot].astype(jnp.float32)
+        send[across(step)] = chunk_sum.astype(jnp.bfloat16)
+        scatter(step).start()
+    for step in (3, 2):
+        scatter(step).start()
+    sent = (1, 2, 3, 4, 6)
+    for step in sent:
         scatter(step).wait_recv()
         total = total + recv[step].astype(jnp.float32)
 
@@ -231,10 +260,12 @@
     for r in range(recv_rows):
         pair_keep = jnp.where(source == sta * recv_rows + r, 0.0, keep)
         out_ref[r] = total[r * stations : (r + 1) * stations] * pair_keep
-    for step in order:
+    for step in range(sta_count):
         swap(step).wait_send()
-        if step:
-            scatter(step).wait_send()
+    for slot in range(2):
+        beside(slot).wait_send()
+    for step in sent:
+        scatter(step).wait_send()
 
 
 def fused(phases, window_valid, freq_taper, pair_mask):
@@ -268,6 +299,10 @@
             vmem((sta_count, block, half), bf16),
             vmem((sta_count, block, half), bf16),
             vmem((sta_count, block, half), bf16),
+            vmem((2, block, half), bf16),
+            vmem((2, block, half), bf16),
+            pltpu.SemaphoreType.DMA((2,)),
+            pltpu.SemaphoreType.DMA((2,)),
             pltpu.SemaphoreType.DMA((sta_count,)),
             pltpu.SemaphoreType.DMA((sta_count,)),
             pltpu.SemaphoreType.DMA((sta_count,)),
@@ -350,8 +385,8 @@
     def body(phases, window_valid, freq_taper, pair_mask):
         win_rows, band, stations = phases.shape
         sta_count, win_count = mesh.shape["sta"], mesh.shape["win"]
-        power = band * sta_count & (band * sta_count - 1) == 0 and sta_count & (sta_count - 1) == 0
-        if band % 128 == 0 and stations % 16 == 0 and win_count == 2 and power:
+        power = band * sta_count & (band * sta_count - 1) == 0
+        if sta_count == 8 and band % 128 == 0 and stations % 16 == 0 and win_count == 2 and power:
             return fused(phases, window_valid, freq_taper, pair_mask)
         return per_device(phases, window_valid, freq_taper, pair_mask)
 

time: 12.2 us -> 14.2 us (1.16)
  Pallas kernels: 11.4 us -> 13.4 us
    pallas_call x1, Pallas kernels: 11.4 us -> 13.4 us  [fused(): pl.pallas_call(lambda *refs: fused_kernel(*refs, sta_count=sta_count), na...]
where the time goes in v4:
time: 14.2 us; the launch traced here: 14 us
  Pallas kernels  13.4 us (94%)
  local copies, waits for them, and re-layouts  0.62 us (4%)
    pallas_call x1, Pallas kernels, fused(): pl.pallas_call(lambda *refs: fused_kernel(*refs, sta_count=sta_count), na...  13.4 us
    unnamed x1, local copies, waits for them, and re-layouts  0.62 us

profile of v4, /device:TPU:0, one launch (start us, length us, event | category | flops | bytes accessed | tf_op | source)
XLA Modules:
  0.0 14.0 jit_solution(948681557783419066)
XLA Ops:
  0.0 13.4 %fused.1 = f32[2,16,256]{2,1,0:T(8,128)S(1)} custom-call(bf16[12,16,256]{2,1,0:T(8,128)(2,1)} %bitcast.2, s32[24]{0:T(128)} %refs_1_.1, f32[16,128]{1,0:T(8,128)} %bitcast.3, s32[8,8]{1,0:T(8,128)} %refs_3_.1), custom_call_target="tpu_custom_call" | custom-call | tf_op jit(solution)/shard_map/fused/pallas_call | solution.py:279
  13.4 0.6 %copy.6 = f32[2,16,256]{2,1,0:T(8,128)} copy(f32[2,16,256]{2,1,0:T(8,128)S(1)} %fused.1) | data formatting | bytes 65536

commit v5 on v3

--- a/solution.py
+++ b/solution.py
@@ -90,7 +90,11 @@
         load.start()
     def across(step):
         bits = [2**n for n in range((sta_count - 1).bit_length())]
-        return sum(lax.rem(lax.div(sta, n) + lax.div(jnp.int32(step), n), 2) * n for n in bits)
+        flips = bits[1::-1] + bits[2:]
+        return sum(
+            lax.rem(lax.div(sta, n) + lax.div(jnp.int32(step), m), 2) * n
+            for n, m in zip(bits, flips)
+        )
 
     barrier = pltpu.get_barrier_semaphore()
     for step in range(sta_count - 1, 0, -1):
@@ -121,8 +125,7 @@
     for load in loads:
         load.wait()
 
-    @pl.loop(0, win_rows)
-    def _(w):
+    for w in range(win_rows):
         weight = valid_ref[win * win_rows + w].astype(jnp.float32)
         c, s = cos_sin(phases_ref[w].astype(jnp.float32))
         cos_ref[w] = c.astype(jnp.bfloat16).astype(jnp.float32) * weight

time: 12.2 us -> 12.1 us (level)
    pallas_call x1, Pallas kernels: 11.4 us -> 11.3 us  [fused(): pl.pallas_call(lambda *refs: fused_kernel(*refs, sta_count=sta_count), na...]
where the time goes in v5:
time: 12.1 us; the launch traced here: 11.9 us
  Pallas kernels  11.3 us (93%)
  local copies, waits for them, and re-layouts  0.62 us (5%)
    pallas_call x1, Pallas kernels, fused(): pl.pallas_call(lambda *refs: fused_kernel(*refs, sta_count=sta_count), na...  11.3 us
    unnamed x1, local copies, waits for them, and re-layouts  0.62 us

profile of v5, /device:TPU:0, one launch (start us, length us, event | category | flops | bytes accessed | tf_op | source)
XLA Modules:
  0.0 11.9 jit_solution(13702443170412942015)
XLA Ops:
  0.0 11.3 %fused.1 = f32[2,16,256]{2,1,0:T(8,128)S(1)} custom-call(bf16[12,16,256]{2,1,0:T(8,128)(2,1)} %bitcast.2, s32[24]{0:T(128)} %refs_1_.1, f32[16,128]{1,0:T(8,128)} %bitcast.3, s32[8,8]{1,0:T(8,128)} %refs_3_.1), custom_call_target="tpu_custom_call" | custom-call | tf_op jit(solution)/shard_map/fused/pallas_call | solution.py:251
  11.3 0.6 %copy.6 = f32[2,16,256]{2,1,0:T(8,128)} copy(f32[2,16,256]{2,1,0:T(8,128)S(1)} %fused.1) | data formatting | bytes 65536

commit v6 on v3

--- a/solution.py
+++ b/solution.py
@@ -121,8 +121,7 @@
     for load in loads:
         load.wait()
 
-    @pl.loop(0, win_rows)
-    def _(w):
+    for w in range(win_rows):
         weight = valid_ref[win * win_rows + w].astype(jnp.float32)
         c, s = cos_sin(phases_ref[w].astype(jnp.float32))
         cos_ref[w] = c.astype(jnp.bfloat16).astype(jnp.float32) * weight
@@ -200,7 +199,7 @@
     pack(0, *lax.fori_loop(1, sta_count, chunk, cross(sta_count - 1)))
     mine = to_lags(spec_re[...], spec_im[...], win)
     swap(0).start()
-    order = range(sta_count - 1, -1, -1)
+    order = (7, 5, 3, 6, 4, 1, 2, 0)
     for b in range(sta_count):
         own[b] = mine[b * block : (b + 1) * block]
 
@@ -351,7 +350,7 @@
         win_rows, band, stations = phases.shape
         sta_count, win_count = mesh.shape["sta"], mesh.shape["win"]
         power = band * sta_count & (band * sta_count - 1) == 0 and sta_count & (sta_count - 1) == 0
-        if band % 128 == 0 and stations % 16 == 0 and win_count == 2 and power:
+        if sta_count == 8 and band % 128 == 0 and stations % 16 == 0 and win_count == 2 and power:
             return fused(phases, window_valid, freq_taper, pair_mask)
         return per_device(phases, window_valid, freq_taper, pair_mask)
 

time: 12.2 us -> 12.1 us (level)
    pallas_call x1, Pallas kernels: 11.4 us -> 11.3 us  [fused(): pl.pallas_call(lambda *refs: fused_kernel(*refs, sta_count=sta_count), na...]
where the time goes in v6:
time: 12.1 us; the launch traced here: 11.9 us
  Pallas kernels  11.3 us (93%)
  local copies, waits for them, and re-layouts  0.62 us (5%)
    pallas_call x1, Pallas kernels, fused(): pl.pallas_call(lambda *refs: fused_kernel(*refs, sta_count=sta_count), na...  11.3 us
    unnamed x1, local copies, waits for them, and re-layouts  0.62 us

profile of v6, /device:TPU:0, one launch (start us, length us, event | category | flops | bytes accessed | tf_op | source)
XLA Modules:
  0.0 11.9 jit_solution(4700040480763864187)
XLA Ops:
  0.0 11.3 %fused.1 = f32[2,16,256]{2,1,0:T(8,128)S(1)} custom-call(bf16[12,16,256]{2,1,0:T(8,128)(2,1)} %bitcast.2, s32[24]{0:T(128)} %refs_1_.1, f32[16,128]{1,0:T(8,128)} %bitcast.3, s32[8,8]{1,0:T(8,128)} %refs_3_.1), custom_call_target="tpu_custom_call" | custom-call | tf_op jit(solution)/shard_map/fused/pallas_call | solution.py:247
  11.3 0.6 %copy.6 = f32[2,16,256]{2,1,0:T(8,128)} copy(f32[2,16,256]{2,1,0:T(8,128)S(1)} %fused.1) | data formatting | bytes 65536
